TPU v7x, 32 devices: a whole 2x2x4 slice. The times are simulated.
32 devices in a mesh: dp: 2 (over x), feat: 16 (over z, y, core).
Axes of the slice: x: 2, y: 2, z: 4, core: 2. Of those that a mesh axis runs over, the one named last changes fastest.
Arguments:
- inputs: bfloat16 [1024, 8192], P('dp', 'feat'), may hold values from -6 to 6
- bfly: bfloat16 [64, 7, 128, 512], P('feat'), may hold values from -0.1875 to 0.1875
- lr_u: bfloat16 [8192, 256], P('feat'), may hold values from -0.0625 to 0.0625
- lr_v: bfloat16 [256, 32768], P(None, 'feat'), may hold values from -0.375 to 0.375
- cotangent: bfloat16 [1024, 32768], P('dp', 'feat'), may hold values from -6 to 6
Outputs:
- activated: bfloat16 [1024, 32768], P('dp', 'feat')
- d_inputs: bfloat16 [1024, 8192], P('dp', 'feat')
- d_bfly: float32 [64, 7, 128, 512], P('feat')
- d_u: float32 [8192, 256], P('feat')
- d_v: float32 [256, 32768], P(None, 'feat')
All inputs are finite; a program needn't handle non-finite values.
Results may differ from a plain program's by a relative error of at most 0.0065.
Values may be sent and summed in bfloat16 or wider, within the bound.
No kernel may reach another device: no remote copies, remote signals or barrier semaphores. Data moves between devices by JAX's collectives and lax.ppermute only.
A program may use at most 128 MiB of HBM per device.

v0:
```python
import jax
import jax.numpy as jnp
from jax import lax
from jax.sharding import PartitionSpec as P


def swapped(block, axis, distance):
    count = lax.axis_size(axis)
    route = []
    for low in range(count):
        high = low | 1 << distance
        if high != low and high < count:
            route += [(low, high), (high, low)]
    return lax.ppermute(block, axis, route)


def gelu_tanh(value):
    return jax.nn.gelu(value, approximate=True)


def flip_blocks(array, step):
    lead = array.shape[0]
    count = array.shape[1]
    rest = array.shape[2:]
    split = array.reshape((lead, count // (2 * step), 2, step) + rest)
    return split[:, :, ::-1].reshape(array.shape)


def local(inputs, bfly, lr_u, lr_v, cotangent):
    tokens = inputs.shape[0]
    per_dev = bfly.shape[0]
    sections = bfly.shape[1]
    width = bfly.shape[2]
    group = bfly.shape[3]
    levels = sections - 1
    local_bits = per_dev.bit_length() - 1
    blocks = inputs.reshape(tokens, per_dev, width)

    def fetch_input(section):
        if 1 << section < per_dev:
            return flip_blocks(blocks, 1 << section)
        return swapped(blocks, "feat", section - local_bits)

    partners = [fetch_input(section) for section in range(levels)] + [blocks]
    butterfly = jnp.zeros((tokens, per_dev, group), jnp.float32)
    for section in range(sections):
        butterfly = butterfly + jnp.einsum(
            "tbi,bio->tbo", partners[section], bfly[:, section], preferred_element_type=jnp.float32
        )
    low = lax.psum(jnp.dot(inputs, lr_u, preferred_element_type=jnp.float32), "feat").astype(
        jnp.bfloat16
    )
    pre = butterfly.reshape(tokens, per_dev * group) + jnp.dot(
        low, lr_v, preferred_element_type=jnp.float32
    )
    activated, backward = jax.vjp(gelu_tanh, pre)
    d_pre = backward(cotangent.astype(jnp.float32))[0].astype(jnp.bfloat16)
    d_low = lax.psum(jnp.dot(d_pre, lr_v.T, preferred_element_type=jnp.float32), "feat").astype(
        jnp.bfloat16
    )
    grad_groups = d_pre.reshape(tokens, per_dev, group)
    d_inputs = jnp.dot(d_low, lr_u.T, preferred_element_type=jnp.float32).reshape(
        tokens, per_dev, width
    )
    for section in range(sections):
        if section == levels:
            term = jnp.einsum(
                "tbo,bio->tbi", grad_groups, bfly[:, section], preferred_element_type=jnp.float32
            ).astype(jnp.bfloat16)
        else:
            mine = jnp.einsum(
                "tbo,bio->tbi", grad_groups, bfly[:, section], preferred_element_type=jnp.float32
            ).astype(jnp.bfloat16)
            if 1 << section < per_dev:
                term = flip_blocks(mine, 1 << section)
            else:
                term = swapped(mine, "feat", section - local_bits)
        d_inputs = d_inputs + lax.optimization_barrier(term).astype(jnp.float32)
    tiles = [
        jnp.einsum(
            "tbi,tbo->bio", partners[section], grad_groups, preferred_element_type=jnp.float32
        )
        for section in range(sections)
    ]
    d_bfly = jnp.stack(tiles, axis=1)
    d_u = jnp.dot(inputs.T, d_low, preferred_element_type=jnp.float32)
    d_v = jnp.dot(low.T, d_pre, preferred_element_type=jnp.float32)
    d_bfly, d_u, d_v = lax.psum((d_bfly, d_u, d_v), "dp")
    scale = 1.0 / jnp.sqrt(jnp.float32(tokens * lax.axis_size("dp")))
    return (
        activated.astype(jnp.bfloat16),
        d_inputs.reshape(tokens, per_dev * width).astype(jnp.bfloat16),
        d_bfly * scale,
        d_u * scale,
        d_v * scale,
    )


def solution(mesh):
    return jax.shard_map(
        local,
        mesh=mesh,
        in_specs=(
            P("dp", "feat"),
            P("feat", None, None, None),
            P("feat", None),
            P(None, "feat"),
            P("dp", "feat"),
        ),
        out_specs=(
            P("dp", "feat"),
            P("dp", "feat"),
            P("feat", None, None, None),
            P("feat", None),
            P(None, "feat"),
        ),
        check_vma=False,
    )
```

profile of v0, /device:TPU:0, one launch (start us, length us, event | category | flops | bytes accessed | tf_op | source)
XLA Modules:
  0.0 474.9 jit_solution(3302909418055266698)
XLA Ops:
  7.2 1.3 copy.49
  9.6 3.0 collective-permute-start.2
  12.6 1.5 collective-permute-start.1
  14.1 2.6 collective-permute-start.3
  16.7 2.0 reshape_reshape.7
  18.7 2.0 reshape_reshape.6
  20.6 3.8 fusion.23
  24.4 2.2 rev.13
  26.6 1.1 copy.47
  28.5 3.8 fusion.40
  32.4 5.6 %rev.12 = bf16[512,2,2,1,128]{4,2,1,0,3:T(2,128)(2,1)} reverse(bf16[512,2,2,1,128]{4,2,1,0,3:T(2,128)(2,1)} %reshape_reshape.6), dimensions={2} | reverse | bytes 1048576 | tf_op jit(solution)/shard_map/rev | solution.py:26
  38.0 1.1 copy.45
  39.2 1.1 fusion.65
  40.3 3.9 fusion.43
  44.2 63.2 %all-reduce.6 = bf16[512,256]{1,0:T(8,128)(2,1)S(1)} all-reduce(f32[512,256]{1,0:T(8,128)S(1)} %copy-done.23), channel_id=1, replica_groups=mesh['dp'=2,'feat'=16] {'feat'}, use_global_device_ids=true, to_apply=%region_0.0 | all-reduce | flops 131072 | bytes 786432 | tf_op jit(solution)/shard_map/psum | solution.py:50
  107.4 2.0 fusion.31
  109.5 2.0 fusion.34
  111.5 4.0 fusion.37
  115.6 6.4 %add_add_fusion = f32[4,512,512]{2,1,0:T(8,128)} fusion(f32[4,512,512]{2,1,0:T(8,128)S(1)} %copy-done.2, f32[4,512,512]{2,1,0:T(8,128)S(1)} %fusion.31, f32[4,512,512]{2,1,0:T(8,128)S(1)} %fusion.34, f32[4,512,512]{2,1,0:T(8,128)} %fusion.37, f32[4,512,512]{2,1,0:T(8,128)S(1)} %copy-done.4, f32[4,512,512]{2,1,0:T(8,128)S(1)} %copy-done.3, ...), kind=kOutput, calls=%fused_computation.14 | convolution fusion | flops 274726912 | bytes 30408704 | tf_op jit(solution)/shard_map/tbi,bio->tbo/dot_general | solution.py:47
  122.0 5.6 %copy.59 = f32[512,2048]{1,0:T(8,128)} copy(f32[512,2048]{0,1:T(8,128)} %bitcast.176) | data formatting | bytes 8388608 | tf_op jit(solution)/shard_map/reshape | solution.py:53
  127.6 6.7 %fusion.2 = (bf16[512,2048]{1,0:T(8,128)(2,1)}, bf16[512,2048]{1,0:T(8,128)(2,1)}) fusion(bf16[512,2048]{1,0:T(8,128)(2,1)S(1)} %copy-done.27, f32[512,2048]{1,0:T(8,128)} %copy.59, bf16[512,256]{1,0:T(8,128)(2,1)S(1)} %all-reduce.6, bf16[256,2048]{1,0:T(8,128)(2,1)S(1)} %copy-done), kind=kOutput, calls=%fused_computation.6 | convolution fusion | flops 562036736 | bytes 11796480 | tf_op jit(solution)/shard_map/dot_general | solution.py:53
  134.4 2.9 copy.103
  137.3 3.9 fusion.68
  141.1 1.5 fusion.66
  142.7 1.7 fusion.16
  144.4 1.7 fusion.15
  146.1 1.7 fusion.14
  147.7 1.7 fusion.13
  149.4 1.7 fusion.12
  151.1 2.8 fusion.11
  153.9 1.7 fusion.10
  155.6 63.6 %all-reduce.7 = bf16[512,256]{1,0:T(8,128)(2,1)S(1)} all-reduce(f32[512,256]{1,0:T(8,128)} %fusion.66), channel_id=1, replica_groups=mesh['dp'=2,'feat'=16] {'feat'}, use_global_device_ids=true, to_apply=%region_1.0 | all-reduce | flops 131072 | bytes 786432 | tf_op jit(solution)/shard_map/psum | solution.py:58
  219.2 1.1 convolution_bitcast_fusion.7
  220.3 2.8 fusion.17
  223.1 2.9 fusion.18
  225.9 2.7 fusion.19
  228.7 2.7 fusion.20
  231.4 1.5 collective-permute-start.7
  232.9 1.9 convolution_convert_fusion.6
  235.7 2.0 convolution_convert_fusion.5
  238.6 2.7 fusion.21
  242.0 7.4 %collective-permute-done.6 = bf16[512,4,128]{2,0,1:T(8,128)(2,1)} collective-permute-done((bf16[512,4,128]{2,0,1:T(8,128)(2,1)}, bf16[512,4,128]{2,0,1:T(8,128)(2,1)}, u32[]{:S(2)}, u32[]{:S(2)}) %collective-permute-start.6) | collective-permute-done | bytes 524320 | tf_op jit(solution)/shard_map/ppermute | solution.py:14
  249.4 8.8 %collective-permute-done.7 = bf16[512,4,128]{2,0,1:T(8,128)(2,1)} collective-permute-done((bf16[512,4,128]{2,0,1:T(8,128)(2,1)}, bf16[512,4,128]{2,0,1:T(8,128)(2,1)}, u32[]{:S(2)}, u32[]{:S(2)}) %collective-permute-start.7) | collective-permute-done | bytes 524320 | tf_op jit(solution)/shard_map/ppermute | solution.py:14
  258.2 2.2 add_convert_fusion
  261.6 189.0 %all-reduce.5.cloned.1.call-done = (f32[4,7,128,512]{2,3,0,1:T(8,128)}, f32[512,256]{0,1:T(8,128)}, f32[256,2048]{1,0:T(8,128)}) async-done(((f32[4,7,128,512]{2,3,0,1:T(8,128)}, f32[512,256]{0,1:T(8,128)}, f32[256,2048]{1,0:T(8,128)}), (f32[4,7,128,512]{2,3,0,1:T(8,128)}, f32[512,256]{0,1:T(8,128)}, f32[256,2048]{1,0:T(8,128)})) %all-reduce.5.cloned.1.call-update) | async-done | bytes 9961488 | tf_op jit(solution)/shard_map/psum | solution.py:88
  450.7 6.8 %broadcast_multiply_fusion = f32[4,7,128,512]{2,3,0,1:T(8,128)} fusion(f32[4,7,128,512]{2,3,0,1:T(8,128)} %get-tuple-element.15), kind=kLoop, calls=%fused_computation.16 | loop fusion | flops 1835008 | bytes 14680064 | tf_op jit(solution)/shard_map/mul | solution.py:93
  457.5 8.1 %copy.85 = f32[4,7,128,512]{3,2,1,0:T(8,128)} copy(f32[4,7,128,512]{2,3,0,1:T(8,128)} %broadcast_multiply_fusion) | data formatting | bytes 14680064
  465.6 1.5 broadcast_multiply_fusion.1
  (77 shorter events, 6.6 us)
Async XLA Ops:
  7.2 120.5 %copy-start = (bf16[256,2048]{1,0:T(8,128)(2,1)S(1)}, bf16[256,2048]{1,0:T(8,128)(2,1)}, u32[]{:S(2)}) copy-start(bf16[256,2048]{1,0:T(8,128)(2,1)} %param.8) | copy-start | bytes 3145732
  7.2 443.5 %all-reduce.5.cloned.1.call-start = ((), (), s32[]{:S(2)}) async-start(), calls=%async_computation | async-start | bytes 19922944 | tf_op jit(solution)/shard_map/psum | solution.py:88
  8.6 15.9 %copy-start.7 = (bf16[512,512]{0,1:T(8,128)(2,1)}, bf16[512,512]{0,1:T(8,128)(2,1)S(1)}, u32[]{:S(2)}) copy-start(bf16[512,512]{0,1:T(8,128)(2,1)S(1)} %copy.49) | copy-start | bytes 1572868
  9.6 97.8 %collective-permute-start.2 = (bf16[512,4,128]{2,0,1:T(8,128)(2,1)}, bf16[512,4,128]{2,0,1:T(8,128)(2,1)S(1)}, u32[]{:S(2)}, u32[]{:S(2)}) collective-permute-start(bf16[512,4,128]{2,0,1:T(8,128)(2,1)} %copy.50), channel_id=1, source_target_pairs={{0,4},{4,0},{1,5},{5,1},{2,6},{6,2},{3,7},{7,3},{8,12},{12,8},{9,1... | collective-permute-start | bytes 1572872 | tf_op jit(solution)/shard_map/ppermute | solution.py:14
  12.6 96.9 %collective-permute-start.1 = (bf16[512,4,128]{2,0,1:T(8,128)(2,1)}, bf16[512,4,128]{2,0,1:T(8,128)(2,1)S(1)}, u32[]{:S(2)}, u32[]{:S(2)}) collective-permute-start(bf16[512,4,128]{2,0,1:T(8,128)(2,1)} %copy.50), channel_id=1, source_target_pairs={{0,2},{2,0},{1,3},{3,1},{4,6},{6,4},{5,7},{7,5},{8,10},{10,8},{9,1... | collective-permute-start | bytes 1572872 | tf_op jit(solution)/shard_map/ppermute | solution.py:14
  14.1 97.4 %collective-permute-start = (bf16[512,4,128]{2,0,1:T(8,128)(2,1)}, bf16[512,4,128]{2,0,1:T(8,128)(2,1)S(1)}, u32[]{:S(2)}, u32[]{:S(2)}) collective-permute-start(bf16[512,4,128]{2,0,1:T(8,128)(2,1)} %copy.50), channel_id=1, source_target_pairs={{0,1},{1,0},{2,3},{3,2},{4,5},{5,4},{6,7},{7,6},{8,9},{9,8},{10,11... | collective-permute-start | bytes 1572872 | tf_op jit(solution)/shard_map/ppermute | solution.py:14
  14.1 101.5 %collective-permute-start.3 = (bf16[512,4,128]{2,0,1:T(8,128)(2,1)}, bf16[512,4,128]{2,0,1:T(8,128)(2,1)}, u32[]{:S(2)}, u32[]{:S(2)}) collective-permute-start(bf16[512,4,128]{2,0,1:T(8,128)(2,1)} %copy.50), channel_id=1, source_target_pairs={{0,8},{8,0},{1,9},{9,1},{2,10},{10,2},{3,11},{11,3},{4,12},{12,4},... | collective-permute-start | bytes 1572872 | tf_op jit(solution)/shard_map/ppermute | solution.py:14
  27.8 0.8 copy-start.10
  28.5 10.6 %copy-start.5 = (bf16[512,512]{1,0:T(8,128)(2,1)S(1)}, bf16[512,512]{1,0:T(8,128)(2,1)}, u32[]{:S(2)}) copy-start(bf16[512,512]{1,0:T(8,128)(2,1)} %param.5) | copy-start | bytes 1572868
  28.5 10.6 %copy-start.24 = (bf16[512,256]{1,0:T(8,128)(2,1)S(1)}, bf16[512,256]{1,0:T(8,128)(2,1)}, u32[]{:S(2)}) copy-start(bf16[512,256]{1,0:T(8,128)(2,1)} %param.7) | copy-start | bytes 786436
  39.2 1.1 copy-start.18
  40.3 3.9 copy-start.23
  107.4 4.1 copy-start.12
  107.4 8.2 %copy-start.4 = (f32[4,512,512]{2,1,0:T(8,128)S(1)}, f32[4,512,512]{2,1,0:T(8,128)}, u32[]{:S(2)}) copy-start(f32[4,512,512]{2,1,0:T(8,128)} %fusion.43) | copy-start | bytes 12582916
  109.5 6.1 %copy-start.14 = (bf16[512,4,128]{2,0,1:T(8,128)(2,1)}, bf16[512,4,128]{2,0,1:T(8,128)(2,1)S(1)}, u32[]{:S(2)}) copy-start(bf16[512,4,128]{2,0,1:T(8,128)(2,1)S(1)} %collective-permute-done.1) | copy-start | bytes 1572868
  109.5 6.1 %copy-start.3 = (f32[4,512,512]{2,1,0:T(8,128)S(1)}, f32[4,512,512]{2,1,0:T(8,128)}, u32[]{:S(2)}) copy-start(f32[4,512,512]{2,1,0:T(8,128)} %fusion.40) | copy-start | bytes 12582916
  111.5 4.1 copy-start.2
  111.5 10.5 %copy-start.16 = (bf16[512,4,128]{2,0,1:T(8,128)(2,1)}, bf16[512,4,128]{2,0,1:T(8,128)(2,1)S(1)}, u32[]{:S(2)}) copy-start(bf16[512,4,128]{2,0,1:T(8,128)(2,1)S(1)} %collective-permute-done) | copy-start | bytes 1572868
  122.0 5.6 %copy-start.27 = (bf16[512,2048]{1,0:T(8,128)(2,1)S(1)}, bf16[512,2048]{1,0:T(8,128)(2,1)}, u32[]{:S(2)}) copy-start(bf16[512,2048]{1,0:T(8,128)(2,1)} %param.9) | copy-start | bytes 6291460
  137.3 3.9 copy-start.9
  141.1 1.5 copy-start.19
  141.1 3.2 copy-start.11
  142.7 3.4 copy-start.17
  144.4 3.4 copy-start.15
  146.1 3.4 copy-start.13
  149.4 4.5 copy-start.8
  151.1 68.0 %copy-start.6 = (bf16[512,512]{1,0:T(8,128)(2,1)S(1)}, bf16[512,512]{1,0:T(8,128)(2,1)}, u32[]{:S(2)}) copy-start(bf16[512,512]{1,0:T(8,128)(2,1)} %param.5) | copy-start | bytes 1572868
  223.1 18.9 %collective-permute-start.4 = (bf16[512,4,128]{2,0,1:T(8,128)(2,1)}, bf16[512,4,128]{2,0,1:T(8,128)(2,1)}, u32[]{:S(2)}, u32[]{:S(2)}) collective-permute-start(bf16[512,4,128]{2,0,1:T(8,128)(2,1)} %fusion.17), channel_id=1, source_target_pairs={{0,1},{1,0},{2,3},{3,2},{4,5},{5,4},{6,7},{7,6},{8,9},{9,8},{10,11... | collective-permute-start | bytes 1572872 | tf_op jit(solution)/shard_map/ppermute | solution.py:14
  225.9 16.1 %collective-permute-start.5 = (bf16[512,4,128]{2,0,1:T(8,128)(2,1)}, bf16[512,4,128]{2,0,1:T(8,128)(2,1)}, u32[]{:S(2)}, u32[]{:S(2)}) collective-permute-start(bf16[512,4,128]{2,0,1:T(8,128)(2,1)} %fusion.18), channel_id=1, source_target_pairs={{0,2},{2,0},{1,3},{3,1},{4,6},{6,4},{5,7},{7,5},{8,10},{10,8},{9,1... | collective-permute-start | bytes 1572872 | tf_op jit(solution)/shard_map/ppermute | solution.py:14
  228.7 20.8 %collective-permute-start.6 = (bf16[512,4,128]{2,0,1:T(8,128)(2,1)}, bf16[512,4,128]{2,0,1:T(8,128)(2,1)}, u32[]{:S(2)}, u32[]{:S(2)}) collective-permute-start(bf16[512,4,128]{2,0,1:T(8,128)(2,1)} %fusion.19), channel_id=1, source_target_pairs={{0,4},{4,0},{1,5},{5,1},{2,6},{6,2},{3,7},{7,3},{8,12},{12,8},{9,1... | collective-permute-start | bytes 1572872 | tf_op jit(solution)/shard_map/ppermute | solution.py:14
  231.4 26.8 %collective-permute-start.7 = (bf16[512,4,128]{2,0,1:T(8,128)(2,1)}, bf16[512,4,128]{2,0,1:T(8,128)(2,1)}, u32[]{:S(2)}, u32[]{:S(2)}) collective-permute-start(bf16[512,4,128]{2,0,1:T(8,128)(2,1)} %fusion.20), channel_id=1, source_target_pairs={{0,8},{8,0},{1,9},{9,1},{2,10},{10,2},{3,11},{11,3},{4,12},{12,4},... | collective-permute-start | bytes 1572872 | tf_op jit(solution)/shard_map/ppermute | solution.py:14
  235.7 5.6 %copy-start.25 = (bf16[512,256]{1,0:T(8,128)(2,1)S(1)}, bf16[512,256]{1,0:T(8,128)(2,1)}, u32[]{:S(2)}) copy-start(bf16[512,256]{1,0:T(8,128)(2,1)} %param.7) | copy-start | bytes 786436
  241.3 16.9 %copy-start.20 = (bf16[512,1,2,2,128]{4,0,3,2,1:T(8,128)(2,1)S(1)}, bf16[512,1,2,2,128]{4,0,3,2,1:T(8,128)(2,1)}, u32[]{:S(2)}) copy-start(bf16[512,1,2,2,128]{4,0,3,2,1:T(8,128)(2,1)} %rev.15) | copy-start | bytes 1572868
  241.3 16.9 %copy-start.22 = (bf16[512,4,128]{2,0,1:T(8,128)(2,1)S(1)}, bf16[512,4,128]{2,0,1:T(8,128)(2,1)}, u32[]{:S(2)}) copy-start(bf16[512,4,128]{2,0,1:T(8,128)(2,1)} %fusion.21) | copy-start | bytes 1572868
  457.5 8.1 %copy-start.21 = (f32[256,2048]{1,0:T(8,128)S(1)}, f32[256,2048]{1,0:T(8,128)}, u32[]{:S(2)}) copy-start(f32[256,2048]{1,0:T(8,128)} %get-tuple-element.17) | copy-start | bytes 6291460
  457.5 10.6 %copy-start.1 = (bf16[256,2048]{1,0:T(8,128)(2,1)S(1)}, bf16[256,2048]{1,0:T(8,128)(2,1)}, u32[]{:S(2)}) copy-start(bf16[256,2048]{1,0:T(8,128)(2,1)} %param.8) | copy-start | bytes 3145732
  465.5 1.5 copy-start.26
Sparse Core Ops, SparseCore 0:
  220.4 230.2 all-reduce.4
where the time goes:
time: 476 us; the launch traced here: 475 us
  waiting for transfers between devices  205 us (43%)
  blocking collectives  127 us (27%)
  matrix products  71.3 us (15%)
  local copies, waits for them, and re-layouts  38 us (8%)
  between operations  14.3 us (3%)
  other arithmetic  10.5 us (2%)
  starting transfers between devices  8.7 us (2%)
    psum x1, waiting for transfers between devices, local(): d_bfly, d_u, d_v = lax.psum((d_bfly, d_u, d_v), 'dp')  189 us
    psum x1, blocking collectives, local(): lax.psum(jnp.dot(d_pre, lr_v.T, preferred_element_type=jnp.float32), 'feat')  63.6 us
    psum x1, blocking collectives, local(): lax.psum(jnp.dot(inputs, lr_u, preferred_element_type=jnp.float32), 'feat')  63.2 us
    dot_general x7, matrix products, local(): jnp.einsum('tbi,bio->tbo', partners[section], bfly[:, section], preferred...  26 us
    dot_general x7, matrix products, local(): jnp.einsum('tbo,bio->tbi', grad_groups, bfly[:, section], preferred_eleme...  17.8 us
    ppermute x8, waiting for transfers between devices, swapped(): return lax.ppermute(block, axis, route)  16.2 us
    dot_general x7, matrix products, local(): jnp.einsum('tbi,tbo->bio', partners[section], grad_groups, preferred_elem...  12.9 us
    unnamed x60, local copies, waits for them, and re-layouts  12.3 us
  transfers between devices with their start and end apart: 9, of which 3 were waited for; matrix products, arithmetic and copies ran while one was open for 12% of the time, Pallas kernels for 0%

commit v1 on v0

--- a/solution.py
+++ b/solution.py
@@ -47,9 +47,9 @@
         butterfly = butterfly + jnp.einsum(
             "tbi,bio->tbo", partners[section], bfly[:, section], preferred_element_type=jnp.float32
         )
-    low = lax.psum(jnp.dot(inputs, lr_u, preferred_element_type=jnp.float32), "feat").astype(
-        jnp.bfloat16
-    )
+    low = jnp.sum(
+        lax.all_gather(jnp.dot(inputs, lr_u, preferred_element_type=jnp.float32), "feat"), axis=0
+    ).astype(jnp.bfloat16)
     pre = butterfly.reshape(tokens, per_dev * group) + jnp.dot(
         low, lr_v, preferred_element_type=jnp.float32
     )

time: 476 us -> 461 us (0.968)
  blocking collectives: 127 us -> 64.9 us
  waiting for transfers between devices: 205 us -> 255 us
  local copies, waits for them, and re-layouts: 38 us -> 30.8 us
    psum x1 -> x0, blocking collectives: 63.2 us -> none  [local(): lax.psum(jnp.dot(inputs, lr_u, preferred_element_type=jnp.float32), 'feat')]
    all_gather x0 -> x1, waiting for transfers between devices: none -> 35.6 us  [local(): lax.all_gather(jnp.dot(inputs, lr_u, preferred_element_type=jnp.float32),...]
    ppermute x8, waiting for transfers between devices: 16.2 us -> 30.2 us  [swapped(): return lax.ppermute(block, axis, route)]
    unnamed x60 -> x50, local copies, waits for them, and re-layouts: 12.3 us -> 11.4 us
  transfers between devices with their start and end apart: 9 -> 10, of which waited for: 3 -> 6; matrix products, arithmetic and copies ran while one was open for 12% -> 14% of each run, Pallas kernels for 0% -> 0%
where the time goes in v1:
time: 461 us; the launch traced here: 460 us
  waiting for transfers between devices  255 us (55%)
  matrix products  71.9 us (16%)
  blocking collectives  64.9 us (14%)
  local copies, waits for them, and re-layouts  30.8 us (7%)
  other arithmetic  14.6 us (3%)
  between operations  14.3 us (3%)
  starting transfers between devices  8.73 us (2%)
    psum x1, waiting for transfers between devices, local(): d_bfly, d_u, d_v = lax.psum((d_bfly, d_u, d_v), 'dp')  189 us
    psum x1, blocking collectives, local(): lax.psum(jnp.dot(d_pre, lr_v.T, preferred_element_type=jnp.float32), 'feat')  64.9 us
    all_gather x1, waiting for transfers between devices, local(): lax.all_gather(jnp.dot(inputs, lr_u, preferred_element_type=jnp.float32),...  35.6 us
    ppermute x8, waiting for transfers between devices, swapped(): return lax.ppermute(block, axis, route)  30.2 us
    dot_general x7, matrix products, local(): jnp.einsum('tbi,bio->tbo', partners[section], bfly[:, section], preferred...  24.3 us
    dot_general x7, matrix products, local(): jnp.einsum('tbo,bio->tbi', grad_groups, bfly[:, section], preferred_eleme...  17.8 us
    dot_general x7, matrix products, local(): jnp.einsum('tbi,tbo->bio', partners[section], grad_groups, preferred_elem...  14 us
    unnamed x50, local copies, waits for them, and re-layouts  11.4 us
  transfers between devices with their start and end apart: 10, of which 6 were waited for; matrix products, arithmetic and copies ran while one was open for 14% of the time, Pallas kernels for 0%

profile of v1, /device:TPU:0, one launch (start us, length us, event | category | flops | bytes accessed | tf_op | source)
XLA Modules:
  0.0 460.1 jit_solution(787300190548293282)
XLA Ops:
  7.2 2.3 fusion.65
  9.6 1.3 copy.49
  11.9 3.0 collective-permute-start.2
  14.9 1.5 collective-permute-start.1
  16.4 2.6 collective-permute-start.3
  20.0 2.2 rev.13
  22.2 1.2 copy.47
  23.3 4.0 fusion.23
  27.4 3.8 fusion.40
  31.3 2.7 rev.12
  34.1 2.0 fusion.43
  36.1 11.4 %collective-permute-done.2 = bf16[512,4,128]{2,0,1:T(8,128)(2,1)S(1)} collective-permute-done((bf16[512,4,128]{2,0,1:T(8,128)(2,1)}, bf16[512,4,128]{2,0,1:T(8,128)(2,1)S(1)}, u32[]{:S(2)}, u32[]{:S(2)}) %collective-permute-start.2) | collective-permute-done | bytes 524320 | tf_op jit(solution)/shard_map/ppermute | solution.py:14
  47.5 2.0 fusion.31
  49.5 2.0 fusion.34
  51.6 4.1 fusion.37
  55.7 2.6 collective-permute-done.3
  58.3 6.4 %add_add_fusion = f32[4,512,512]{2,1,0:T(8,128)} fusion(f32[4,512,512]{2,1,0:T(8,128)S(1)} %copy-done.2, f32[4,512,512]{2,1,0:T(8,128)S(1)} %fusion.31, f32[4,512,512]{2,1,0:T(8,128)S(1)} %fusion.34, f32[4,512,512]{2,1,0:T(8,128)} %fusion.37, f32[4,512,512]{2,1,0:T(8,128)S(1)} %fusion.43, f32[4,512,512]{2,1,0:T(8,128)S(1)} %copy-done.3, ...), kind=kOutput, calls=%fused_computation.14 | convolution fusion | flops 274726912 | bytes 30408704 | tf_op jit(solution)/shard_map/tbi,bio->tbo/dot_general | solution.py:47
  64.7 5.9 %copy.59 = f32[512,2048]{1,0:T(8,128)} copy(f32[512,2048]{0,1:T(8,128)} %bitcast.177) | data formatting | bytes 8388608 | tf_op jit(solution)/shard_map/reshape | solution.py:53
  70.5 35.6 %all-gather.3.cloned.1.call-done = f32[8192,256]{1,0:T(8,128)} async-done(((f32[512,256]{1,0:T(8,128)}), f32[8192,256]{1,0:T(8,128)}) %all-gather.3.cloned.1.call-update) | async-done | bytes 8388624 | tf_op jit(solution)/shard_map/all_gather | solution.py:51
  106.2 4.1 reduce_sum.9
  110.3 6.8 %fusion.2 = (bf16[512,2048]{1,0:T(8,128)(2,1)}, bf16[512,2048]{1,0:T(8,128)(2,1)}) fusion(bf16[512,2048]{1,0:T(8,128)(2,1)S(1)} %copy-done.22, f32[512,2048]{1,0:T(8,128)} %copy.59, bf16[512,256]{1,0:T(8,128)(2,1)S(1)} %reduce_sum.9, bf16[256,2048]{1,0:T(8,128)(2,1)S(1)} %copy-done), kind=kOutput, calls=%fused_computation.6 | convolution fusion | flops 562036736 | bytes 11796480 | tf_op jit(solution)/shard_map/dot_general | solution.py:53
  117.1 3.0 copy.103
  120.1 3.9 fusion.68
  124.0 1.5 fusion.66
  125.5 1.7 fusion.16
  127.2 1.7 fusion.15
  128.9 2.8 fusion.14
  131.7 1.7 fusion.13
  133.4 1.7 fusion.12
  135.0 2.8 fusion.11
  137.8 1.7 fusion.10
  139.5 64.9 %all-reduce.5 = bf16[512,256]{1,0:T(8,128)(2,1)S(1)} all-reduce(f32[512,256]{1,0:T(8,128)} %fusion.66), channel_id=1, replica_groups=mesh['dp'=2,'feat'=16] {'feat'}, use_global_device_ids=true, to_apply=%region_1.0 | all-reduce | flops 131072 | bytes 786432 | tf_op jit(solution)/shard_map/psum | solution.py:58
  204.4 1.1 convolution_bitcast_fusion.7
  205.5 2.8 fusion.17
  208.3 2.9 fusion.18
  211.2 2.7 fusion.19
  213.9 2.7 fusion.20
  216.7 1.5 collective-permute-start.7
  218.2 1.9 convolution_convert_fusion.6
  221.0 2.0 convolution_convert_fusion.5
  223.8 2.7 fusion.21
  227.2 7.4 %collective-permute-done.6 = bf16[512,4,128]{2,0,1:T(8,128)(2,1)} collective-permute-done((bf16[512,4,128]{2,0,1:T(8,128)(2,1)}, bf16[512,4,128]{2,0,1:T(8,128)(2,1)}, u32[]{:S(2)}, u32[]{:S(2)}) %collective-permute-start.6) | collective-permute-done | bytes 524320 | tf_op jit(solution)/shard_map/ppermute | solution.py:14
  234.7 8.8 %collective-permute-done.7 = bf16[512,4,128]{2,0,1:T(8,128)(2,1)} collective-permute-done((bf16[512,4,128]{2,0,1:T(8,128)(2,1)}, bf16[512,4,128]{2,0,1:T(8,128)(2,1)}, u32[]{:S(2)}, u32[]{:S(2)}) %collective-permute-start.7) | collective-permute-done | bytes 524320 | tf_op jit(solution)/shard_map/ppermute | solution.py:14
  243.5 2.2 add_convert_fusion
  246.9 188.9 %all-reduce.4.cloned.1.call-done = (f32[4,7,128,512]{2,3,0,1:T(8,128)}, f32[512,256]{0,1:T(8,128)}, f32[256,2048]{1,0:T(8,128)}) async-done(((f32[4,7,128,512]{2,3,0,1:T(8,128)}, f32[512,256]{0,1:T(8,128)}, f32[256,2048]{1,0:T(8,128)}), (f32[4,7,128,512]{2,3,0,1:T(8,128)}, f32[512,256]{0,1:T(8,128)}, f32[256,2048]{1,0:T(8,128)})) %all-reduce.4.cloned.1.call-update) | async-done | bytes 9961488 | tf_op jit(solution)/shard_map/psum | solution.py:88
  435.8 6.8 %broadcast_multiply_fusion = f32[4,7,128,512]{2,3,0,1:T(8,128)} fusion(f32[4,7,128,512]{2,3,0,1:T(8,128)} %get-tuple-element.15), kind=kLoop, calls=%fused_computation.16 | loop fusion | flops 1835008 | bytes 14680064 | tf_op jit(solution)/shard_map/mul | solution.py:93
  442.7 8.1 %copy.85 = f32[4,7,128,512]{3,2,1,0:T(8,128)} copy(f32[4,7,128,512]{2,3,0,1:T(8,128)} %broadcast_multiply_fusion) | data formatting | bytes 14680064
  450.7 1.5 broadcast_multiply_fusion.1
  (70 shorter events, 6.9 us)
Async XLA Ops:
  7.2 103.1 %copy-start = (bf16[256,2048]{1,0:T(8,128)(2,1)S(1)}, bf16[256,2048]{1,0:T(8,128)(2,1)}, u32[]{:S(2)}) copy-start(bf16[256,2048]{1,0:T(8,128)(2,1)} %param.8) | copy-start | bytes 3145732
  7.2 11.9 %copy-start.4 = (bf16[512,512]{1,0:T(8,128)(2,1)S(1)}, bf16[512,512]{1,0:T(8,128)(2,1)}, u32[]{:S(2)}) copy-start(bf16[512,512]{1,0:T(8,128)(2,1)} %param.5) | copy-start | bytes 1572868
  7.2 99.0 %all-gather.3.cloned.1.call-start = ((), (), s32[]{:S(2)}) async-start(), calls=%async_computation | async-start | bytes 8912896 | tf_op jit(solution)/shard_map/all_gather | solution.py:51
  9.6 426.2 %all-reduce.4.cloned.1.call-start = ((), (), s32[]{:S(2)}) async-start(), calls=%async_computation.1 | async-start | bytes 19922944 | tf_op jit(solution)/shard_map/psum | solution.py:88
  10.9 16.5 %copy-start.6 = (bf16[512,512]{0,1:T(8,128)(2,1)}, bf16[512,512]{0,1:T(8,128)(2,1)S(1)}, u32[]{:S(2)}) copy-start(bf16[512,512]{0,1:T(8,128)(2,1)S(1)} %copy.49) | copy-start | bytes 1572868
  11.9 35.6 %collective-permute-start.2 = (bf16[512,4,128]{2,0,1:T(8,128)(2,1)}, bf16[512,4,128]{2,0,1:T(8,128)(2,1)S(1)}, u32[]{:S(2)}, u32[]{:S(2)}) collective-permute-start(bf16[512,4,128]{2,0,1:T(8,128)(2,1)} %copy.50), channel_id=1, source_target_pairs={{0,4},{4,0},{1,5},{5,1},{2,6},{6,2},{3,7},{7,3},{8,12},{12,8},{9,1... | collective-permute-start | bytes 1572872 | tf_op jit(solution)/shard_map/ppermute | solution.py:14
  14.9 34.6 %collective-permute-start.1 = (bf16[512,4,128]{2,0,1:T(8,128)(2,1)}, bf16[512,4,128]{2,0,1:T(8,128)(2,1)S(1)}, u32[]{:S(2)}, u32[]{:S(2)}) collective-permute-start(bf16[512,4,128]{2,0,1:T(8,128)(2,1)} %copy.50), channel_id=1, source_target_pairs={{0,2},{2,0},{1,3},{3,1},{4,6},{6,4},{5,7},{7,5},{8,10},{10,8},{9,1... | collective-permute-start | bytes 1572872 | tf_op jit(solution)/shard_map/ppermute | solution.py:14
  16.4 35.1 %collective-permute-start = (bf16[512,4,128]{2,0,1:T(8,128)(2,1)}, bf16[512,4,128]{2,0,1:T(8,128)(2,1)}, u32[]{:S(2)}, u32[]{:S(2)}) collective-permute-start(bf16[512,4,128]{2,0,1:T(8,128)(2,1)} %copy.50), channel_id=1, source_target_pairs={{0,1},{1,0},{2,3},{3,2},{4,5},{5,4},{6,7},{7,6},{8,9},{9,8},{10,11... | collective-permute-start | bytes 1572872 | tf_op jit(solution)/shard_map/ppermute | solution.py:14
  16.4 41.8 %collective-permute-start.3 = (bf16[512,4,128]{2,0,1:T(8,128)(2,1)}, bf16[512,4,128]{2,0,1:T(8,128)(2,1)}, u32[]{:S(2)}, u32[]{:S(2)}) collective-permute-start(bf16[512,4,128]{2,0,1:T(8,128)(2,1)} %copy.50), channel_id=1, source_target_pairs={{0,8},{8,0},{1,9},{9,1},{2,10},{10,2},{3,11},{11,3},{4,12},{12,4},... | collective-permute-start | bytes 1572872 | tf_op jit(solution)/shard_map/ppermute | solution.py:14
  23.3 4.0 copy-start.9
  34.1 2.0 copy-start.15
  47.5 4.1 copy-start.11
  49.5 6.1 %copy-start.13 = (bf16[512,4,128]{2,0,1:T(8,128)(2,1)}, bf16[512,4,128]{2,0,1:T(8,128)(2,1)S(1)}, u32[]{:S(2)}) copy-start(bf16[512,4,128]{2,0,1:T(8,128)(2,1)S(1)} %collective-permute-done.1) | copy-start | bytes 1572868
  49.5 8.8 %copy-start.3 = (f32[4,512,512]{2,1,0:T(8,128)S(1)}, f32[4,512,512]{2,1,0:T(8,128)}, u32[]{:S(2)}) copy-start(f32[4,512,512]{2,1,0:T(8,128)} %fusion.40) | copy-start | bytes 12582916
  51.6 6.7 %copy-start.2 = (f32[4,512,512]{2,1,0:T(8,128)S(1)}, f32[4,512,512]{2,1,0:T(8,128)}, u32[]{:S(2)}) copy-start(f32[4,512,512]{2,1,0:T(8,128)} %fusion.23) | copy-start | bytes 12582916
  106.2 4.1 copy-start.22
  120.1 3.9 copy-start.8
  124.0 1.5 copy-start.16
  124.0 3.2 copy-start.10
  127.2 4.5 copy-start.14
  128.9 4.5 copy-start.12
  133.4 4.5 copy-start.7
  135.0 69.3 %copy-start.5 = (bf16[512,512]{1,0:T(8,128)(2,1)S(1)}, bf16[512,512]{1,0:T(8,128)(2,1)}, u32[]{:S(2)}) copy-start(bf16[512,512]{1,0:T(8,128)(2,1)} %param.5) | copy-start | bytes 1572868
  208.3 18.9 %collective-permute-start.4 = (bf16[512,4,128]{2,0,1:T(8,128)(2,1)}, bf16[512,4,128]{2,0,1:T(8,128)(2,1)}, u32[]{:S(2)}, u32[]{:S(2)}) collective-permute-start(bf16[512,4,128]{2,0,1:T(8,128)(2,1)} %fusion.17), channel_id=1, source_target_pairs={{0,1},{1,0},{2,3},{3,2},{4,5},{5,4},{6,7},{7,6},{8,9},{9,8},{10,11... | collective-permute-start | bytes 1572872 | tf_op jit(solution)/shard_map/ppermute | solution.py:14
  211.2 16.0 %collective-permute-start.5 = (bf16[512,4,128]{2,0,1:T(8,128)(2,1)}, bf16[512,4,128]{2,0,1:T(8,128)(2,1)}, u32[]{:S(2)}, u32[]{:S(2)}) collective-permute-start(bf16[512,4,128]{2,0,1:T(8,128)(2,1)} %fusion.18), channel_id=1, source_target_pairs={{0,2},{2,0},{1,3},{3,1},{4,6},{6,4},{5,7},{7,5},{8,10},{10,8},{9,1... | collective-permute-start | bytes 1572872 | tf_op jit(solution)/shard_map/ppermute | solution.py:14
  213.9 20.8 %collective-permute-start.6 = (bf16[512,4,128]{2,0,1:T(8,128)(2,1)}, bf16[512,4,128]{2,0,1:T(8,128)(2,1)}, u32[]{:S(2)}, u32[]{:S(2)}) collective-permute-start(bf16[512,4,128]{2,0,1:T(8,128)(2,1)} %fusion.19), channel_id=1, source_target_pairs={{0,4},{4,0},{1,5},{5,1},{2,6},{6,2},{3,7},{7,3},{8,12},{12,8},{9,1... | collective-permute-start | bytes 1572872 | tf_op jit(solution)/shard_map/ppermute | solution.py:14
  216.7 26.8 %collective-permute-start.7 = (bf16[512,4,128]{2,0,1:T(8,128)(2,1)}, bf16[512,4,128]{2,0,1:T(8,128)(2,1)}, u32[]{:S(2)}, u32[]{:S(2)}) collective-permute-start(bf16[512,4,128]{2,0,1:T(8,128)(2,1)} %fusion.20), channel_id=1, source_target_pairs={{0,8},{8,0},{1,9},{9,1},{2,10},{10,2},{3,11},{11,3},{4,12},{12,4},... | collective-permute-start | bytes 1572872 | tf_op jit(solution)/shard_map/ppermute | solution.py:14
  221.0 5.6 %copy-start.20 = (bf16[512,256]{1,0:T(8,128)(2,1)S(1)}, bf16[512,256]{1,0:T(8,128)(2,1)}, u32[]{:S(2)}) copy-start(bf16[512,256]{1,0:T(8,128)(2,1)} %param.7) | copy-start | bytes 786436
  226.5 16.9 %copy-start.17 = (bf16[512,1,2,2,128]{4,0,3,2,1:T(8,128)(2,1)S(1)}, bf16[512,1,2,2,128]{4,0,3,2,1:T(8,128)(2,1)}, u32[]{:S(2)}) copy-start(bf16[512,1,2,2,128]{4,0,3,2,1:T(8,128)(2,1)} %rev.15) | copy-start | bytes 1572868
  226.5 16.9 %copy-start.19 = (bf16[512,4,128]{2,0,1:T(8,128)(2,1)S(1)}, bf16[512,4,128]{2,0,1:T(8,128)(2,1)}, u32[]{:S(2)}) copy-start(bf16[512,4,128]{2,0,1:T(8,128)(2,1)} %fusion.21) | copy-start | bytes 1572868
  442.7 8.1 %copy-start.18 = (f32[256,2048]{1,0:T(8,128)S(1)}, f32[256,2048]{1,0:T(8,128)}, u32[]{:S(2)}) copy-start(f32[256,2048]{1,0:T(8,128)} %get-tuple-element.17) | copy-start | bytes 6291460
  442.7 10.6 %copy-start.1 = (bf16[256,2048]{1,0:T(8,128)(2,1)S(1)}, bf16[256,2048]{1,0:T(8,128)(2,1)}, u32[]{:S(2)}) copy-start(bf16[256,2048]{1,0:T(8,128)(2,1)} %param.8) | copy-start | bytes 3145732
  450.7 1.5 copy-start.21
Sparse Core Ops, SparseCore 0:
  10.8 95.3 all-gather.2
  205.7 230.1 all-reduce.3
